TPU v7x, 32 devices: a whole 2x2x4 slice. The times are simulated.
32 devices in a mesh: px: 4 (over x, core), py: 8 (over z, y).
Axes of the slice: x: 2, y: 2, z: 4, core: 2. Of those that a mesh axis runs over, the one named last changes fastest.
Arguments:
- fraction: float32 [32, 64, 640], P('px', 'py'), may hold values from 0 to 1
- courant_x: float32 [32, 64, 640], P('px', 'py'), may hold values from -0.5 to 0.5
- courant_y: float32 [32, 64, 640], P('px', 'py'), may hold values from -0.5 to 0.5
- courant_z: float32 [32, 64, 640], P('px', 'py'), may hold values from -0.5 to 0.5
- labels: int32 [32, 64, 640], P('px', 'py'), may hold values from -1 to 31, as said below
- structure_owner: int32 [4, 32], P('px'), may hold values from 0 to 7, as said below
- parcel_owner: int32 [4, 32], P('px'), may hold values from 0 to 7, as said below
Outputs:
- remaining: float32 [32, 64, 640], P('px', 'py')
- moments: float32 [4, 13, 32], P('px', None, 'py')
- parcels: float32 [4, 13, 32], P('px', None, 'py')
Inputs may be any that keep to these rules, and one draw needn't show every extreme that they name: `labels`: a label names a structure of the cell's row. `structure_owner`: in each row every index of py owns exactly 4 structures. `parcel_owner`: in each row every index of py receives exactly 4 parcels.
All inputs are finite; a program needn't handle non-finite values.
Results may differ from a plain program's by a relative error of at most 0.0003.
Values sent between devices are 32-bit elements; how exact they have to be, the bound alone decides.
A program may use at most 64 MiB of HBM per device.

v0:
```python
import math
import jax
import jax.numpy as jnp
from jax import lax
from jax.sharding import PartitionSpec as P


def with_halo(x, sides, width, wrap):
    for axis, dim in sides:
        size, length = (lax.axis_size(axis), x.shape[dim])
        up = [(i, (i + 1) % size) for i in range(size if wrap else size - 1)]
        down = [(j, i) for i, j in up]
        last = lax.slice_in_dim(x, length - width, length, axis=dim)
        initial = lax.slice_in_dim(x, 0, width, axis=dim)
        before = lax.ppermute(last, axis, up)
        after = lax.ppermute(initial, axis, down)
        x = jnp.concatenate([before, x, after], axis=dim)
    return x


def advance(padded_frac, padded_cour, length, axis):

    def part(array, start, count):
        return lax.slice_in_dim(array, start, start + count, axis=axis)

    centre = part(padded_frac, 1, length + 2)
    spread = 0.5 * (part(padded_frac, 2, length + 2) - part(padded_frac, 0, length + 2))
    bound = 2.0 * jnp.minimum(centre, 1.0 - centre)
    slope = jnp.minimum(jnp.maximum(spread, -bound), bound)
    courant = part(padded_cour, 1, length + 1)
    upwind = part(centre, 0, length + 1) + 0.5 * (1.0 - courant) * part(slope, 0, length + 1)
    downwind = part(centre, 1, length + 1) - 0.5 * (1.0 + courant) * part(slope, 1, length + 1)
    flux = courant * jnp.where(courant > 0.0, upwind, downwind)
    middle = part(padded_frac, 2, length)
    high = part(courant, 1, length)
    low = part(courant, 0, length)
    updated = middle - (part(flux, 1, length) - part(flux, 0, length)) + middle * (high - low)
    return (updated, 0.5 * (high + low))


def parcel_rows(moment_rows):
    volume = moment_rows[0]
    safe = jnp.maximum(volume, 0.5)
    centre = moment_rows[1:4] / safe
    velocity = moment_rows[4:7] / safe
    square = moment_rows[7:10] / safe - centre * centre
    cross = jnp.stack(
        [
            moment_rows[10] / safe - centre[0] * centre[1],
            moment_rows[11] / safe - centre[0] * centre[2],
            moment_rows[12] / safe - centre[1] * centre[2],
        ]
    )
    return jnp.concatenate([volume[None], centre, velocity, square, cross], 0)


def slot_table(owner_row, per_owner):
    count = owner_row.shape[0]
    index = jnp.arange(count, dtype=jnp.int32)
    same = owner_row[:, None] == owner_row[None, :]
    earlier = index[None, :] < index[:, None]
    rank = jnp.sum((same & earlier).astype(jnp.int32), axis=1)
    position = owner_row * per_owner + rank
    return (position[:, None] == index[None, :]).astype(jnp.float32)


def product(left, right):
    return jnp.dot(left, right, precision=lax.Precision.HIGHEST, preferred_element_type=jnp.float32)


def local(fraction, courant_x, courant_y, courant_z, labels, structure_owner, parcel_owner):
    rows_x, rows_y, depth = fraction.shape
    padded = with_halo(jnp.stack([fraction, courant_x]), (("px", 1),), 2, True)
    first, velocity_x = advance(padded[0], padded[1], rows_x, 0)
    padded_y = with_halo(jnp.stack([first, courant_y]), (("py", 2),), 2, False)
    second, velocity_y = advance(padded_y[0], padded_y[1], rows_y, 1)
    pad_z = ((0, 0), (0, 0), (2, 2))
    third, velocity_z = advance(jnp.pad(second, pad_z), jnp.pad(courant_z, pad_z), depth, 2)
    remaining = jnp.where(labels >= 0, jnp.float32(0.0), third)
    width_py = lax.axis_size("py")
    row_index = lax.axis_index("py")
    total_x = rows_x * lax.axis_size("px")
    total_y = rows_y * width_py
    structures = structure_owner.shape[1]
    per_owner = structures // width_py
    scale = 4.0 / (rows_x * rows_y * rows_y)
    start_x = lax.axis_index("px") * rows_x
    start_y = row_index * rows_y
    coord_x = ((start_x + jnp.arange(rows_x, dtype=jnp.int32)).astype(jnp.float32) + 0.5)[
        :, None, None
    ] / total_x
    coord_y = ((start_y + jnp.arange(rows_y, dtype=jnp.int32)).astype(jnp.float32) + 0.5)[
        None, :, None
    ] / total_y
    coord_z = (jnp.arange(depth, dtype=jnp.int32).astype(jnp.float32) + 0.5)[None, None, :] / depth
    weight = third * scale
    shape = weight.shape
    cells = rows_x * rows_y * depth
    block = math.gcd(cells, 4096)
    blocks = cells // block
    pieces = [
        jnp.ones(shape, jnp.float32),
        coord_x,
        coord_y,
        coord_z,
        velocity_x,
        velocity_y,
        velocity_z,
        coord_x * coord_x,
        coord_y * coord_y,
        coord_z * coord_z,
        coord_x * coord_y,
        coord_x * coord_z,
        coord_y * coord_z,
    ]
    feature_blocks = jnp.stack(
        [(weight * jnp.broadcast_to(piece, shape)).reshape(blocks, block) for piece in pieces], 1
    )
    label_blocks = labels.reshape(blocks, block)
    columns = jnp.arange(structures, dtype=jnp.int32)

    def accumulate(total, inputs):
        feature_rows, marks = inputs
        onehot = (marks[:, None] == columns[None, :]).astype(jnp.float32)
        return (total + product(feature_rows, onehot), None)

    partial_sums, unused = lax.scan(
        accumulate, jnp.zeros((13, structures), jnp.float32), (feature_blocks, label_blocks)
    )
    owner_slots = slot_table(structure_owner[0], per_owner)
    parcel_slots = slot_table(parcel_owner[0], per_owner)
    mine_owned = lax.dynamic_slice_in_dim(owner_slots, row_index * per_owner, per_owner, 1)
    totals = lax.psum(partial_sums, "py")
    owned = product(totals, mine_owned)
    mine_parcels = lax.dynamic_slice_in_dim(parcel_slots, row_index * per_owner, per_owner, 1)
    received = product(parcel_rows(totals), mine_parcels)
    return (remaining, owned[None], received[None])


def solution(mesh):
    return jax.shard_map(
        local,
        mesh=mesh,
        in_specs=(
            P("px", "py", None),
            P("px", "py", None),
            P("px", "py", None),
            P("px", "py", None),
            P("px", "py", None),
            P("px", None),
            P("px", None),
        ),
        out_specs=(P("px", "py", None), P("px", None, "py"), P("px", None, "py")),
        check_vma=False,
    )
```

profile of v0, /device:TPU:0, one launch (start us, length us, event | category | flops | bytes accessed | tf_op | source)
XLA Modules:
  0.0 86.4 jit_solution(18232538209815463961)
XLA Ops:
  0.7 0.9 %pad_maximum_fusion.7 = (f32[2,2,8,640]{3,2,1,0:T(8,128)S(1)}, f32[2,2,8,640]{3,2,1,0:T(8,128)S(1)}) fusion(f32[1,8,8,640]{3,2,1,0:T(8,128)} %bitcast.59, f32[1,8,8,640]{3,2,1,0:T(8,128)} %bitcast.63), kind=kLoop, calls=%fused_computation.82 | loop fusion | flops 40960 | bytes 491520 | tf_op jit(solution)/shard_map/stack | solution.py:73
  1.6 2.5 %collective-permute-start.1 = (f32[2,2,8,640]{3,2,1,0:T(8,128)S(1)}, f32[2,2,8,640]{3,2,1,0:T(8,128)S(1)}, u32[]{:S(2)}, u32[]{:S(2)}) collective-permute-start(f32[2,2,8,640]{3,2,1,0:T(8,128)S(1)} %get-tuple-element.72), channel_id=1, source_target_pairs={{8,0},{16,8},{24,16},{0,24},{9,1},{17,9},{25,17},{1,25},{10,2},{18... | collective-permute-start | bytes 245768 | tf_op jit(solution)/shard_map/ppermute | solution.py:16
  4.2 1.7 %reshape.154 = s32[10,4096]{1,0:T(8,128)} reshape(s32[8,8,640]{2,1,0:T(8,128)} %param.13) | data formatting | bytes 327680 | tf_op jit(solution)/shard_map/reshape | solution.py:119
  5.9 0.9 %convert_reduce_fusion = s32[32]{0:T(128)S(1)} fusion(s32[32]{0:T(128)} %bitcast.70), kind=kLoop, calls=%fused_computation.112 | loop fusion | flops 5088 | bytes 256 | tf_op jit(solution)/shard_map/reduce_sum | solution.py:62
  6.8 0.7 multiply_add_fusion
  7.5 0.9 %convert_reduce_fusion.1 = s32[32]{0:T(128)S(1)} fusion(s32[32]{0:T(128)} %bitcast.71), kind=kLoop, calls=%fused_computation.113 | loop fusion | flops 5088 | bytes 256 | tf_op jit(solution)/shard_map/reduce_sum | solution.py:62
  8.4 0.7 multiply_add_fusion.1
  9.0 1.2 %pad_maximum_fusion.1 = (f32[2,10,8,640]{3,2,1,0:T(8,128)S(1)}, f32[2,10,8,640]{3,2,1,0:T(8,128)S(1)}) fusion(f32[2,2,8,640]{3,2,1,0:T(8,128)S(1)} %collective-permute-done.1, f32[1,8,8,640]{3,2,1,0:T(8,128)} %bitcast.60, f32[1,8,8,640]{3,2,1,0:T(8,128)} %bitcast.64, f32[2,2,8,640]{3,2,1,0:T(8,128)S(1)} %collective-permute-done), kind=kLoop, calls=%fused_computation.12 | loop fusion | flops 409600 | bytes 1310720 | tf_op jit(solution)/shard_map/concatenate | solution.py:17
  10.3 1.0 %fusion.16 = f32[10,8,640]{2,1,0:T(8,128)S(1)} fusion(f32[2,10,8,640]{3,2,1,0:T(8,128)S(1)} %get-tuple-element.71, f32[2,10,8,640]{3,2,1,0:T(8,128)S(1)} %get-tuple-element.70, f32[2,2,8,640]{3,2,1,0:T(8,128)S(1)} %collective-permute-done.1, f32[1,8,8,640]{3,2,1,0:T(8,128)} %bitcast.61, f32[1,8,8,640]{3,2,1,0:T(8,128)} %bitcast.65, ...), kind=kLoop, calls=%fused_computation.42 | loop fusion | flops 563200 | bytes 1105920 | tf_op jit(solution)/shard_map/min | solution.py:29
  11.5 3.4 %collective-permute-start.2 = (f32[2,8,2,640]{3,2,1,0:T(2,128)S(1)}, f32[2,8,2,640]{3,2,1,0:T(2,128)S(1)}, u32[]{:S(2)}, u32[]{:S(2)}) collective-permute-start(f32[2,8,2,640]{3,2,1,0:T(2,128)S(1)} %get-tuple-element.68), channel_id=1, source_target_pairs={{0,1},{1,2},{2,3},{3,4},{4,5},{5,6},{6,7},{8,9},{9,10},{10,11},{11... | collective-permute-start | bytes 245768 | tf_op jit(solution)/shard_map/ppermute | solution.py:15
  14.9 1.3 %collective-permute-start.3 = (f32[2,8,2,640]{3,2,1,0:T(2,128)S(1)}, f32[2,8,2,640]{3,2,1,0:T(2,128)S(1)}, u32[]{:S(2)}, u32[]{:S(2)}) collective-permute-start(f32[2,8,2,640]{3,2,1,0:T(2,128)S(1)} %get-tuple-element.69), channel_id=1, source_target_pairs={{1,0},{2,1},{3,2},{4,3},{5,4},{6,5},{7,6},{9,8},{10,9},{11,10},{12... | collective-permute-start | bytes 245768 | tf_op jit(solution)/shard_map/ppermute | solution.py:16
  16.2 1.3 %collective-permute-done.2 = f32[2,8,2,640]{3,2,1,0:T(2,128)S(1)} collective-permute-done((f32[2,8,2,640]{3,2,1,0:T(2,128)S(1)}, f32[2,8,2,640]{3,2,1,0:T(2,128)S(1)}, u32[]{:S(2)}, u32[]{:S(2)}) %collective-permute-start.2) | collective-permute-done | bytes 81952 | tf_op jit(solution)/shard_map/ppermute | solution.py:15
  17.5 4.1 %collective-permute-done.3 = f32[2,8,2,640]{3,2,1,0:T(2,128)S(1)} collective-permute-done((f32[2,8,2,640]{3,2,1,0:T(2,128)S(1)}, f32[2,8,2,640]{3,2,1,0:T(2,128)S(1)}, u32[]{:S(2)}, u32[]{:S(2)}) %collective-permute-start.3) | collective-permute-done | bytes 81952 | tf_op jit(solution)/shard_map/ppermute | solution.py:16
  21.9 0.2 fusion.6
  22.2 0.2 fusion.23
  22.4 0.2 fusion.19
  22.8 0.9 %broadcast_multiply_fusion.1 = (f32[8,8,640]{2,1,0:T(8,128)S(1)}, f32[8,8,640]{2,1,0:T(8,128)S(1)}, f32[8,8,640]{2,1,0:T(8,128)S(1)}, f32[8,8,640]{2,1,0:T(8,128...) fusion(f32[8,8,640]{2,1,0:T(8,128)S(1)} %get-tuple-element.65, ...), kind=kLoop, calls=%fused_computation.85 | loop fusion | flops 819200 | bytes 3302784 | tf_op jit(solution)/shard_map/mul | solution.py:117
  23.7 0.7 constant_dynamic-update-slice_fusion.12
  25.0 0.7 constant_dynamic-update-slice_fusion.11
  25.7 0.7 constant_dynamic-update-slice_fusion.10
  26.4 0.7 constant_dynamic-update-slice_fusion.9
  27.2 0.7 constant_dynamic-update-slice_fusion.8
  27.9 0.7 constant_dynamic-update-slice_fusion.7
  28.6 0.7 constant_dynamic-update-slice_fusion.6
  29.4 0.7 constant_dynamic-update-slice_fusion.5
  30.1 0.7 constant_dynamic-update-slice_fusion.4
  30.8 0.7 constant_dynamic-update-slice_fusion.3
  31.6 0.7 constant_dynamic-update-slice_fusion.2
  32.3 0.7 constant_dynamic-update-slice_fusion.1
  33.0 0.7 constant_dynamic-update-slice_fusion
  33.7 30.6 %while.11 = (s32[]{:T(128)}, f32[13,32]{1,0:T(8,128)S(1)}, f32[10,13,4096]{2,0,1:T(8,128)}, s32[10,4096]{1,0:T(8,128)}, s32[]{:T(128)}, /*index=5*/s32[]{:T(128)}) while((s32[]{:T(128)}, f32[13,32]{1,0:T(8,128)S(1)}, f32[10,13,4096]{2,0,1:T(8,128)}, s32[10,4096]{1,0:T(8,128)}, s32[]{:T(128)}, /*index=5*/s32[]{:T(128)}) %tuple.55), condition=%wide.region_1.2_spmd.clone, body=%wide.region_0.1_spmd.clone.sunk | while | flops 20579140 | bytes 691543 | solution.py:127
  33.7 1.6 %constant_dynamic-slice_fusion.4 = f32[1,13,4096]{2,0,1:T(1,128)S(1)} fusion(f32[10,13,4096]{2,0,1:T(8,128)} %get-tuple-element.143, s32[]{:T(128)} %get-tuple-element.135), kind=kLoop, calls=%fused_computation.6.clone.1 | loop fusion | bytes 425988 | tf_op jit(solution)/shard_map/while/body/jit(dynamic_index_in_dim)/dynamic_slice | solution.py:127
  35.4 0.9 %constant_dynamic-slice_fusion.5 = s32[1,4096]{1,0:T(1,128)S(1)} fusion(s32[10,4096]{1,0:T(8,128)} %get-tuple-element.144, s32[]{:T(128)} %get-tuple-element.135), kind=kLoop, calls=%fused_computation.5.clone.1 | loop fusion | bytes 32772 | tf_op jit(solution)/shard_map/while/body/jit(dynamic_index_in_dim)/dynamic_slice | solution.py:127
  36.3 0.5 convolution_add_fusion.2
  36.8 1.6 %constant_dynamic-slice_fusion.4 = f32[1,13,4096]{2,0,1:T(1,128)S(1)} fusion(f32[10,13,4096]{2,0,1:T(8,128)} %get-tuple-element.143, s32[]{:T(128)} %get-tuple-element.135), kind=kLoop, calls=%fused_computation.6.clone.1 | loop fusion | bytes 425988 | tf_op jit(solution)/shard_map/while/body/jit(dynamic_index_in_dim)/dynamic_slice | solution.py:127
  38.5 0.9 %constant_dynamic-slice_fusion.5 = s32[1,4096]{1,0:T(1,128)S(1)} fusion(s32[10,4096]{1,0:T(8,128)} %get-tuple-element.144, s32[]{:T(128)} %get-tuple-element.135), kind=kLoop, calls=%fused_computation.5.clone.1 | loop fusion | bytes 32772 | tf_op jit(solution)/shard_map/while/body/jit(dynamic_index_in_dim)/dynamic_slice | solution.py:127
  39.4 0.5 convolution_add_fusion.2
  39.9 1.6 %constant_dynamic-slice_fusion.4 = f32[1,13,4096]{2,0,1:T(1,128)S(1)} fusion(f32[10,13,4096]{2,0,1:T(8,128)} %get-tuple-element.143, s32[]{:T(128)} %get-tuple-element.135), kind=kLoop, calls=%fused_computation.6.clone.1 | loop fusion | bytes 425988 | tf_op jit(solution)/shard_map/while/body/jit(dynamic_index_in_dim)/dynamic_slice | solution.py:127
  41.5 0.9 %constant_dynamic-slice_fusion.5 = s32[1,4096]{1,0:T(1,128)S(1)} fusion(s32[10,4096]{1,0:T(8,128)} %get-tuple-element.144, s32[]{:T(128)} %get-tuple-element.135), kind=kLoop, calls=%fused_computation.5.clone.1 | loop fusion | bytes 32772 | tf_op jit(solution)/shard_map/while/body/jit(dynamic_index_in_dim)/dynamic_slice | solution.py:127
  42.5 0.5 convolution_add_fusion.2
  42.9 1.6 %constant_dynamic-slice_fusion.4 = f32[1,13,4096]{2,0,1:T(1,128)S(1)} fusion(f32[10,13,4096]{2,0,1:T(8,128)} %get-tuple-element.143, s32[]{:T(128)} %get-tuple-element.135), kind=kLoop, calls=%fused_computation.6.clone.1 | loop fusion | bytes 425988 | tf_op jit(solution)/shard_map/while/body/jit(dynamic_index_in_dim)/dynamic_slice | solution.py:127
  44.6 0.9 %constant_dynamic-slice_fusion.5 = s32[1,4096]{1,0:T(1,128)S(1)} fusion(s32[10,4096]{1,0:T(8,128)} %get-tuple-element.144, s32[]{:T(128)} %get-tuple-element.135), kind=kLoop, calls=%fused_computation.5.clone.1 | loop fusion | bytes 32772 | tf_op jit(solution)/shard_map/while/body/jit(dynamic_index_in_dim)/dynamic_slice | solution.py:127
  45.5 0.5 convolution_add_fusion.2
  46.0 1.6 %constant_dynamic-slice_fusion.4 = f32[1,13,4096]{2,0,1:T(1,128)S(1)} fusion(f32[10,13,4096]{2,0,1:T(8,128)} %get-tuple-element.143, s32[]{:T(128)} %get-tuple-element.135), kind=kLoop, calls=%fused_computation.6.clone.1 | loop fusion | bytes 425988 | tf_op jit(solution)/shard_map/while/body/jit(dynamic_index_in_dim)/dynamic_slice | solution.py:127
  47.7 0.9 %constant_dynamic-slice_fusion.5 = s32[1,4096]{1,0:T(1,128)S(1)} fusion(s32[10,4096]{1,0:T(8,128)} %get-tuple-element.144, s32[]{:T(128)} %get-tuple-element.135), kind=kLoop, calls=%fused_computation.5.clone.1 | loop fusion | bytes 32772 | tf_op jit(solution)/shard_map/while/body/jit(dynamic_index_in_dim)/dynamic_slice | solution.py:127
  48.6 0.5 convolution_add_fusion.2
  49.1 1.6 %constant_dynamic-slice_fusion.4 = f32[1,13,4096]{2,0,1:T(1,128)S(1)} fusion(f32[10,13,4096]{2,0,1:T(8,128)} %get-tuple-element.143, s32[]{:T(128)} %get-tuple-element.135), kind=kLoop, calls=%fused_computation.6.clone.1 | loop fusion | bytes 425988 | tf_op jit(solution)/shard_map/while/body/jit(dynamic_index_in_dim)/dynamic_slice | solution.py:127
  50.7 0.9 %constant_dynamic-slice_fusion.5 = s32[1,4096]{1,0:T(1,128)S(1)} fusion(s32[10,4096]{1,0:T(8,128)} %get-tuple-element.144, s32[]{:T(128)} %get-tuple-element.135), kind=kLoop, calls=%fused_computation.5.clone.1 | loop fusion | bytes 32772 | tf_op jit(solution)/shard_map/while/body/jit(dynamic_index_in_dim)/dynamic_slice | solution.py:127
  51.7 0.5 convolution_add_fusion.2
  52.1 1.6 %constant_dynamic-slice_fusion.4 = f32[1,13,4096]{2,0,1:T(1,128)S(1)} fusion(f32[10,13,4096]{2,0,1:T(8,128)} %get-tuple-element.143, s32[]{:T(128)} %get-tuple-element.135), kind=kLoop, calls=%fused_computation.6.clone.1 | loop fusion | bytes 425988 | tf_op jit(solution)/shard_map/while/body/jit(dynamic_index_in_dim)/dynamic_slice | solution.py:127
  53.8 0.9 %constant_dynamic-slice_fusion.5 = s32[1,4096]{1,0:T(1,128)S(1)} fusion(s32[10,4096]{1,0:T(8,128)} %get-tuple-element.144, s32[]{:T(128)} %get-tuple-element.135), kind=kLoop, calls=%fused_computation.5.clone.1 | loop fusion | bytes 32772 | tf_op jit(solution)/shard_map/while/body/jit(dynamic_index_in_dim)/dynamic_slice | solution.py:127
  54.7 0.5 convolution_add_fusion.2
  55.2 1.6 %constant_dynamic-slice_fusion.4 = f32[1,13,4096]{2,0,1:T(1,128)S(1)} fusion(f32[10,13,4096]{2,0,1:T(8,128)} %get-tuple-element.143, s32[]{:T(128)} %get-tuple-element.135), kind=kLoop, calls=%fused_computation.6.clone.1 | loop fusion | bytes 425988 | tf_op jit(solution)/shard_map/while/body/jit(dynamic_index_in_dim)/dynamic_slice | solution.py:127
  56.9 0.9 %constant_dynamic-slice_fusion.5 = s32[1,4096]{1,0:T(1,128)S(1)} fusion(s32[10,4096]{1,0:T(8,128)} %get-tuple-element.144, s32[]{:T(128)} %get-tuple-element.135), kind=kLoop, calls=%fused_computation.5.clone.1 | loop fusion | bytes 32772 | tf_op jit(solution)/shard_map/while/body/jit(dynamic_index_in_dim)/dynamic_slice | solution.py:127
  57.8 0.5 convolution_add_fusion.2
  58.3 1.6 %constant_dynamic-slice_fusion.4 = f32[1,13,4096]{2,0,1:T(1,128)S(1)} fusion(f32[10,13,4096]{2,0,1:T(8,128)} %get-tuple-element.143, s32[]{:T(128)} %get-tuple-element.135), kind=kLoop, calls=%fused_computation.6.clone.1 | loop fusion | bytes 425988 | tf_op jit(solution)/shard_map/while/body/jit(dynamic_index_in_dim)/dynamic_slice | solution.py:127
  59.9 0.9 %constant_dynamic-slice_fusion.5 = s32[1,4096]{1,0:T(1,128)S(1)} fusion(s32[10,4096]{1,0:T(8,128)} %get-tuple-element.144, s32[]{:T(128)} %get-tuple-element.135), kind=kLoop, calls=%fused_computation.5.clone.1 | loop fusion | bytes 32772 | tf_op jit(solution)/shard_map/while/body/jit(dynamic_index_in_dim)/dynamic_slice | solution.py:127
  60.9 0.5 convolution_add_fusion.2
  61.3 1.6 %constant_dynamic-slice_fusion.4 = f32[1,13,4096]{2,0,1:T(1,128)S(1)} fusion(f32[10,13,4096]{2,0,1:T(8,128)} %get-tuple-element.143, s32[]{:T(128)} %get-tuple-element.135), kind=kLoop, calls=%fused_computation.6.clone.1 | loop fusion | bytes 425988 | tf_op jit(solution)/shard_map/while/body/jit(dynamic_index_in_dim)/dynamic_slice | solution.py:127
  63.0 0.9 %constant_dynamic-slice_fusion.5 = s32[1,4096]{1,0:T(1,128)S(1)} fusion(s32[10,4096]{1,0:T(8,128)} %get-tuple-element.144, s32[]{:T(128)} %get-tuple-element.135), kind=kLoop, calls=%fused_computation.5.clone.1 | loop fusion | bytes 32772 | tf_op jit(solution)/shard_map/while/body/jit(dynamic_index_in_dim)/dynamic_slice | solution.py:127
  63.9 0.5 convolution_add_fusion.2
  64.4 20.1 %psum.7 = f32[13,32]{1,0:T(8,128)S(1)} all-reduce(f32[13,32]{1,0:T(8,128)S(1)} %get-tuple-element.30), channel_id=1, replica_groups=mesh['px'=4,'py'=8] {'py'}, use_global_device_ids=true, to_apply=%region_2.3 | all-reduce | flops 416 | bytes 3328 | tf_op jit(solution)/shard_map/psum | solution.py:133
  84.6 0.8 convolution_bitcast_fusion.1
  85.5 0.8 convolution_bitcast_fusion
  (46 shorter events, 1.5 us)
Async XLA Ops:
  0.6 10.6 %copy-start.1 = (f32[8,8,640]{2,1,0:T(8,128)S(1)}, f32[8,8,640]{2,1,0:T(8,128)}, u32[]{:S(2)}) copy-start(f32[8,8,640]{2,1,0:T(8,128)} %param.9) | copy-start | bytes 491524
  0.6 10.6 %copy-start = (f32[8,8,640]{2,1,0:T(8,128)S(1)}, f32[8,8,640]{2,1,0:T(8,128)}, u32[]{:S(2)}) copy-start(f32[8,8,640]{2,1,0:T(8,128)} %param.10) | copy-start | bytes 491524
  0.7 10.8 %copy-start.4 = (f32[8,8,640]{2,1,0:T(8,128)S(1)}, f32[8,8,640]{2,1,0:T(8,128)}, u32[]{:S(2)}) copy-start(f32[8,8,640]{2,1,0:T(8,128)} %param.11) | copy-start | bytes 491524
  1.6 7.5 %collective-permute-start.1 = (f32[2,2,8,640]{3,2,1,0:T(8,128)S(1)}, f32[2,2,8,640]{3,2,1,0:T(8,128)S(1)}, u32[]{:S(2)}, u32[]{:S(2)}) collective-permute-start(f32[2,2,8,640]{3,2,1,0:T(8,128)S(1)} %get-tuple-element.72), channel_id=1, source_target_pairs={{8,0},{16,8},{24,16},{0,24},{9,1},{17,9},{25,17},{1,25},{10,2},{18... | collective-permute-start | bytes 245768 | tf_op jit(solution)/shard_map/ppermute | solution.py:16
  4.0 5.0 %collective-permute-start = (f32[2,2,8,640]{3,2,1,0:T(8,128)S(1)}, f32[2,2,8,640]{3,2,1,0:T(8,128)S(1)}, u32[]{:S(2)}, u32[]{:S(2)}) collective-permute-start(f32[2,2,8,640]{3,2,1,0:T(8,128)S(1)} %get-tuple-element.73), channel_id=1, source_target_pairs={{0,8},{8,16},{16,24},{24,0},{1,9},{9,17},{17,25},{25,1},{2,10},{10... | collective-permute-start | bytes 245768 | tf_op jit(solution)/shard_map/ppermute | solution.py:15
  11.5 6.0 %collective-permute-start.2 = (f32[2,8,2,640]{3,2,1,0:T(2,128)S(1)}, f32[2,8,2,640]{3,2,1,0:T(2,128)S(1)}, u32[]{:S(2)}, u32[]{:S(2)}) collective-permute-start(f32[2,8,2,640]{3,2,1,0:T(2,128)S(1)} %get-tuple-element.68), channel_id=1, source_target_pairs={{0,1},{1,2},{2,3},{3,4},{4,5},{5,6},{6,7},{8,9},{9,10},{10,11},{11... | collective-permute-start | bytes 245768 | tf_op jit(solution)/shard_map/ppermute | solution.py:15
  14.9 6.7 %collective-permute-start.3 = (f32[2,8,2,640]{3,2,1,0:T(2,128)S(1)}, f32[2,8,2,640]{3,2,1,0:T(2,128)S(1)}, u32[]{:S(2)}, u32[]{:S(2)}) collective-permute-start(f32[2,8,2,640]{3,2,1,0:T(2,128)S(1)} %get-tuple-element.69), channel_id=1, source_target_pairs={{1,0},{2,1},{3,2},{4,3},{5,4},{6,5},{7,6},{9,8},{10,9},{11,10},{12... | collective-permute-start | bytes 245768 | tf_op jit(solution)/shard_map/ppermute | solution.py:16
  16.2 6.2 %copy-start.2 = (f32[8,8,640]{2,1,0:T(8,128)S(1)}, f32[8,8,640]{2,1,0:T(8,128)}, u32[]{:S(2)}) copy-start(f32[8,8,640]{2,1,0:T(8,128)} %param.12) | copy-start | bytes 491524
  21.8 1.0 %copy-start.3 = (s32[8,8,640]{2,1,0:T(8,128)S(1)}, s32[8,8,640]{2,1,0:T(8,128)}, u32[]{:S(2)}) copy-start(s32[8,8,640]{2,1,0:T(8,128)} %param.13) | copy-start | bytes 491524
where the time goes:
time: 87.1 us; the launch traced here: 86.4 us
  local copies, waits for them, and re-layouts  37.5 us (43%)
  blocking collectives  20.1 us (23%)
  other arithmetic  8.61 us (10%)
  starting transfers between devices  7.18 us (8%)
  matrix products  6.3 us (7%)
  waiting for transfers between devices  5.37 us (6%)
  between operations  0.97 us (1%)
    dynamic_slice x20, local copies, waits for them, and re-layouts, local(): lax.scan(accumulate, jnp.zeros((13, structures), jnp.float32), (feature_b...  25.7 us
    psum x1, blocking collectives, local(): totals = lax.psum(partial_sums, 'py')  20.1 us
    unnamed x22, local copies, waits for them, and re-layouts  8.8 us
    dot_general x12, matrix products, product(): jnp.dot(left, right, precision=lax.Precision.HIGHEST, preferred_element_t...  6.3 us
    ppermute x2, waiting for transfers between devices, with_halo(): after = lax.ppermute(initial, axis, down)  4.12 us
    ppermute x2, starting transfers between devices, with_halo(): after = lax.ppermute(initial, axis, down)  3.75 us
    ppermute x2, starting transfers between devices, with_halo(): before = lax.ppermute(last, axis, up)  3.43 us
    reduce_sum x2, other arithmetic, slot_table(): rank = jnp.sum((same & earlier).astype(jnp.int32), axis=1)  1.82 us
  transfers between devices with their start and end apart: 4, of which 2 were waited for; matrix products, arithmetic and copies ran while one was open for 6% of the time, Pallas kernels for 0%

commit v1 on v0

--- a/solution.py
+++ b/solution.py
@@ -130,7 +130,7 @@
     owner_slots = slot_table(structure_owner[0], per_owner)
     parcel_slots = slot_table(parcel_owner[0], per_owner)
     mine_owned = lax.dynamic_slice_in_dim(owner_slots, row_index * per_owner, per_owner, 1)
-    totals = lax.psum(partial_sums, "py")
+    totals = lax.all_gather(partial_sums, "py").sum(axis=0)
     owned = product(totals, mine_owned)
     mine_parcels = lax.dynamic_slice_in_dim(parcel_slots, row_index * per_owner, per_owner, 1)
     received = product(parcel_rows(totals), mine_parcels)

time: 87.1 us -> 97.9 us (1.12)
  blocking collectives: 20.1 us -> 30.9 us
    all_gather x0 -> x1, blocking collectives: none -> 30.9 us  [local(): totals = lax.all_gather(partial_sums, 'py').sum(axis=0)]
    psum x1 -> x0, blocking collectives: 20.1 us -> none  [local(): totals = lax.psum(partial_sums, 'py')]
  transfers between devices with their start and end apart: 4 -> 4, of which waited for: 2 -> 2; matrix products, arithmetic and copies ran while one was open for 6% -> 5% of each run, Pallas kernels for 0% -> 0%
where the time goes in v1:
time: 97.9 us; the launch traced here: 97.1 us
  local copies, waits for them, and re-layouts  37.5 us (38%)
  blocking collectives  30.9 us (32%)
  other arithmetic  8.62 us (9%)
  starting transfers between devices  7.18 us (7%)
  matrix products  6.3 us (6%)
  waiting for transfers between devices  5.37 us (5%)
    all_gather x1, blocking collectives, local(): totals = lax.all_gather(partial_sums, 'py').sum(axis=0)  30.9 us
    dynamic_slice x20, local copies, waits for them, and re-layouts, local(): lax.scan(accumulate, jnp.zeros((13, structures), jnp.float32), (feature_b...  25.7 us
    unnamed x22, local copies, waits for them, and re-layouts  8.8 us
    dot_general x12, matrix products, product(): jnp.dot(left, right, precision=lax.Precision.HIGHEST, preferred_element_t...  6.3 us
    ppermute x2, waiting for transfers between devices, with_halo(): after = lax.ppermute(initial, axis, down)  4.12 us
    ppermute x2, starting transfers between devices, with_halo(): after = lax.ppermute(initial, axis, down)  3.75 us
    ppermute x2, starting transfers between devices, with_halo(): before = lax.ppermute(last, axis, up)  3.43 us
  transfers between devices with their start and end apart: 4, of which 2 were waited for; matrix products, arithmetic and copies ran while one was open for 5% of the time, Pallas kernels for 0%

profile of v1, /device:TPU:0, one launch (start us, length us, event | category | flops | bytes accessed | tf_op | source)
XLA Modules:
  0.0 97.1 jit_solution(156089805139490663)
XLA Ops:
  0.7 0.9 pad_maximum_fusion.7
  1.6 2.5 %collective-permute-start.1 = (f32[2,2,8,640]{3,2,1,0:T(8,128)S(1)}, f32[2,2,8,640]{3,2,1,0:T(8,128)S(1)}, u32[]{:S(2)}, u32[]{:S(2)}) collective-permute-start(f32[2,2,8,640]{3,2,1,0:T(8,128)S(1)} %get-tuple-element.76), channel_id=1, source_target_pairs={{8,0},{16,8},{24,16},{0,24},{9,1},{17,9},{25,17},{1,25},{10,2},{18... | collective-permute-start | bytes 245768 | tf_op jit(solution)/shard_map/ppermute | solution.py:16
  4.2 1.7 %reshape.154 = s32[10,4096]{1,0:T(8,128)} reshape(s32[8,8,640]{2,1,0:T(8,128)} %param.13) | data formatting | bytes 327680 | tf_op jit(solution)/shard_map/reshape | solution.py:119
  5.9 0.9 convert_reduce_fusion
  6.8 0.7 multiply_add_fusion
  7.5 0.9 convert_reduce_fusion.1
  8.4 0.7 multiply_add_fusion.1
  9.0 1.2 %pad_maximum_fusion.1 = (f32[2,10,8,640]{3,2,1,0:T(8,128)S(1)}, f32[2,10,8,640]{3,2,1,0:T(8,128)S(1)}) fusion(f32[2,2,8,640]{3,2,1,0:T(8,128)S(1)} %collective-permute-done.1, f32[1,8,8,640]{3,2,1,0:T(8,128)} %bitcast.61, f32[1,8,8,640]{3,2,1,0:T(8,128)} %bitcast.65, f32[2,2,8,640]{3,2,1,0:T(8,128)S(1)} %collective-permute-done), kind=kLoop, calls=%fused_computation.12 | loop fusion | flops 409600 | bytes 1310720 | tf_op jit(solution)/shard_map/concatenate | solution.py:17
  10.3 1.0 %fusion.16 = f32[10,8,640]{2,1,0:T(8,128)S(1)} fusion(f32[2,10,8,640]{3,2,1,0:T(8,128)S(1)} %get-tuple-element.75, f32[2,10,8,640]{3,2,1,0:T(8,128)S(1)} %get-tuple-element.74, f32[2,2,8,640]{3,2,1,0:T(8,128)S(1)} %collective-permute-done.1, f32[1,8,8,640]{3,2,1,0:T(8,128)} %bitcast.62, f32[1,8,8,640]{3,2,1,0:T(8,128)} %bitcast.66, ...), kind=kLoop, calls=%fused_computation.42 | loop fusion | flops 563200 | bytes 1105920 | tf_op jit(solution)/shard_map/min | solution.py:29
  11.5 3.4 %collective-permute-start.2 = (f32[2,8,2,640]{3,2,1,0:T(2,128)S(1)}, f32[2,8,2,640]{3,2,1,0:T(2,128)S(1)}, u32[]{:S(2)}, u32[]{:S(2)}) collective-permute-start(f32[2,8,2,640]{3,2,1,0:T(2,128)S(1)} %get-tuple-element.72), channel_id=1, source_target_pairs={{0,1},{1,2},{2,3},{3,4},{4,5},{5,6},{6,7},{8,9},{9,10},{10,11},{11... | collective-permute-start | bytes 245768 | tf_op jit(solution)/shard_map/ppermute | solution.py:15
  14.9 1.3 %collective-permute-start.3 = (f32[2,8,2,640]{3,2,1,0:T(2,128)S(1)}, f32[2,8,2,640]{3,2,1,0:T(2,128)S(1)}, u32[]{:S(2)}, u32[]{:S(2)}) collective-permute-start(f32[2,8,2,640]{3,2,1,0:T(2,128)S(1)} %get-tuple-element.73), channel_id=1, source_target_pairs={{1,0},{2,1},{3,2},{4,3},{5,4},{6,5},{7,6},{9,8},{10,9},{11,10},{12... | collective-permute-start | bytes 245768 | tf_op jit(solution)/shard_map/ppermute | solution.py:16
  16.2 1.3 %collective-permute-done.2 = f32[2,8,2,640]{3,2,1,0:T(2,128)S(1)} collective-permute-done((f32[2,8,2,640]{3,2,1,0:T(2,128)S(1)}, f32[2,8,2,640]{3,2,1,0:T(2,128)S(1)}, u32[]{:S(2)}, u32[]{:S(2)}) %collective-permute-start.2) | collective-permute-done | bytes 81952 | tf_op jit(solution)/shard_map/ppermute | solution.py:15
  17.5 4.1 %collective-permute-done.3 = f32[2,8,2,640]{3,2,1,0:T(2,128)S(1)} collective-permute-done((f32[2,8,2,640]{3,2,1,0:T(2,128)S(1)}, f32[2,8,2,640]{3,2,1,0:T(2,128)S(1)}, u32[]{:S(2)}, u32[]{:S(2)}) %collective-permute-start.3) | collective-permute-done | bytes 81952 | tf_op jit(solution)/shard_map/ppermute | solution.py:16
  21.9 0.2 fusion.6
  22.2 0.2 fusion.23
  22.4 0.2 fusion.19
  22.8 0.9 broadcast_multiply_fusion.1
  23.7 0.7 constant_dynamic-update-slice_fusion.12
  25.0 0.7 constant_dynamic-update-slice_fusion.11
  25.7 0.7 constant_dynamic-update-slice_fusion.10
  26.4 0.7 constant_dynamic-update-slice_fusion.9
  27.2 0.7 constant_dynamic-update-slice_fusion.8
  27.9 0.7 constant_dynamic-update-slice_fusion.7
  28.6 0.7 constant_dynamic-update-slice_fusion.6
  29.4 0.7 constant_dynamic-update-slice_fusion.5
  30.1 0.7 constant_dynamic-update-slice_fusion.4
  30.8 0.7 constant_dynamic-update-slice_fusion.3
  31.6 0.7 constant_dynamic-update-slice_fusion.2
  32.3 0.7 constant_dynamic-update-slice_fusion.1
  33.0 0.7 constant_dynamic-update-slice_fusion
  33.7 30.6 %while.11 = (s32[]{:T(128)}, f32[13,32]{1,0:T(8,128)S(1)}, f32[10,13,4096]{2,0,1:T(8,128)}, s32[10,4096]{1,0:T(8,128)}, s32[]{:T(128)}, /*index=5*/s32[]{:T(128)}) while((s32[]{:T(128)}, f32[13,32]{1,0:T(8,128)S(1)}, f32[10,13,4096]{2,0,1:T(8,128)}, s32[10,4096]{1,0:T(8,128)}, s32[]{:T(128)}, /*index=5*/s32[]{:T(128)}) %tuple.56), condition=%wide.region_1.2_spmd.clone, body=%wide.region_0.1_spmd.clone.sunk | while | flops 20579140 | bytes 691543 | solution.py:127
  33.7 1.6 %constant_dynamic-slice_fusion.4 = f32[1,13,4096]{2,0,1:T(1,128)S(1)} fusion(f32[10,13,4096]{2,0,1:T(8,128)} %get-tuple-element.147, s32[]{:T(128)} %get-tuple-element.139), kind=kLoop, calls=%fused_computation.6.clone.1 | loop fusion | bytes 425988 | tf_op jit(solution)/shard_map/while/body/jit(dynamic_index_in_dim)/dynamic_slice | solution.py:127
  35.4 0.9 constant_dynamic-slice_fusion.5
  36.3 0.5 convolution_add_fusion.2
  36.8 1.6 %constant_dynamic-slice_fusion.4 = f32[1,13,4096]{2,0,1:T(1,128)S(1)} fusion(f32[10,13,4096]{2,0,1:T(8,128)} %get-tuple-element.147, s32[]{:T(128)} %get-tuple-element.139), kind=kLoop, calls=%fused_computation.6.clone.1 | loop fusion | bytes 425988 | tf_op jit(solution)/shard_map/while/body/jit(dynamic_index_in_dim)/dynamic_slice | solution.py:127
  38.5 0.9 constant_dynamic-slice_fusion.5
  39.4 0.5 convolution_add_fusion.2
  39.9 1.6 %constant_dynamic-slice_fusion.4 = f32[1,13,4096]{2,0,1:T(1,128)S(1)} fusion(f32[10,13,4096]{2,0,1:T(8,128)} %get-tuple-element.147, s32[]{:T(128)} %get-tuple-element.139), kind=kLoop, calls=%fused_computation.6.clone.1 | loop fusion | bytes 425988 | tf_op jit(solution)/shard_map/while/body/jit(dynamic_index_in_dim)/dynamic_slice | solution.py:127
  41.5 0.9 constant_dynamic-slice_fusion.5
  42.5 0.5 convolution_add_fusion.2
  42.9 1.6 %constant_dynamic-slice_fusion.4 = f32[1,13,4096]{2,0,1:T(1,128)S(1)} fusion(f32[10,13,4096]{2,0,1:T(8,128)} %get-tuple-element.147, s32[]{:T(128)} %get-tuple-element.139), kind=kLoop, calls=%fused_computation.6.clone.1 | loop fusion | bytes 425988 | tf_op jit(solution)/shard_map/while/body/jit(dynamic_index_in_dim)/dynamic_slice | solution.py:127
  44.6 0.9 constant_dynamic-slice_fusion.5
  45.5 0.5 convolution_add_fusion.2
  46.0 1.6 %constant_dynamic-slice_fusion.4 = f32[1,13,4096]{2,0,1:T(1,128)S(1)} fusion(f32[10,13,4096]{2,0,1:T(8,128)} %get-tuple-element.147, s32[]{:T(128)} %get-tuple-element.139), kind=kLoop, calls=%fused_computation.6.clone.1 | loop fusion | bytes 425988 | tf_op jit(solution)/shard_map/while/body/jit(dynamic_index_in_dim)/dynamic_slice | solution.py:127
  47.7 0.9 constant_dynamic-slice_fusion.5
  48.6 0.5 convolution_add_fusion.2
  49.1 1.6 %constant_dynamic-slice_fusion.4 = f32[1,13,4096]{2,0,1:T(1,128)S(1)} fusion(f32[10,13,4096]{2,0,1:T(8,128)} %get-tuple-element.147, s32[]{:T(128)} %get-tuple-element.139), kind=kLoop, calls=%fused_computation.6.clone.1 | loop fusion | bytes 425988 | tf_op jit(solution)/shard_map/while/body/jit(dynamic_index_in_dim)/dynamic_slice | solution.py:127
  50.7 0.9 constant_dynamic-slice_fusion.5
  51.7 0.5 convolution_add_fusion.2
  52.1 1.6 %constant_dynamic-slice_fusion.4 = f32[1,13,4096]{2,0,1:T(1,128)S(1)} fusion(f32[10,13,4096]{2,0,1:T(8,128)} %get-tuple-element.147, s32[]{:T(128)} %get-tuple-element.139), kind=kLoop, calls=%fused_computation.6.clone.1 | loop fusion | bytes 425988 | tf_op jit(solution)/shard_map/while/body/jit(dynamic_index_in_dim)/dynamic_slice | solution.py:127
  53.8 0.9 constant_dynamic-slice_fusion.5
  54.7 0.5 convolution_add_fusion.2
  55.2 1.6 %constant_dynamic-slice_fusion.4 = f32[1,13,4096]{2,0,1:T(1,128)S(1)} fusion(f32[10,13,4096]{2,0,1:T(8,128)} %get-tuple-element.147, s32[]{:T(128)} %get-tuple-element.139), kind=kLoop, calls=%fused_computation.6.clone.1 | loop fusion | bytes 425988 | tf_op jit(solution)/shard_map/while/body/jit(dynamic_index_in_dim)/dynamic_slice | solution.py:127
  56.9 0.9 constant_dynamic-slice_fusion.5
  57.8 0.5 convolution_add_fusion.2
  58.3 1.6 %constant_dynamic-slice_fusion.4 = f32[1,13,4096]{2,0,1:T(1,128)S(1)} fusion(f32[10,13,4096]{2,0,1:T(8,128)} %get-tuple-element.147, s32[]{:T(128)} %get-tuple-element.139), kind=kLoop, calls=%fused_computation.6.clone.1 | loop fusion | bytes 425988 | tf_op jit(solution)/shard_map/while/body/jit(dynamic_index_in_dim)/dynamic_slice | solution.py:127
  59.9 0.9 constant_dynamic-slice_fusion.5
  60.9 0.5 convolution_add_fusion.2
  61.3 1.6 %constant_dynamic-slice_fusion.4 = f32[1,13,4096]{2,0,1:T(1,128)S(1)} fusion(f32[10,13,4096]{2,0,1:T(8,128)} %get-tuple-element.147, s32[]{:T(128)} %get-tuple-element.139), kind=kLoop, calls=%fused_computation.6.clone.1 | loop fusion | bytes 425988 | tf_op jit(solution)/shard_map/while/body/jit(dynamic_index_in_dim)/dynamic_slice | solution.py:127
  63.0 0.9 constant_dynamic-slice_fusion.5
  63.9 0.5 convolution_add_fusion.2
  64.4 30.9 %all-gather.1 = f32[8,13,32]{2,1,0:T(8,128)S(1)} all-gather(f32[1,13,32]{2,1,0:T(8,128)S(1)} %bitcast.71), channel_id=2, replica_groups=mesh['px'=4,'py'=8] {'py'}, dimensions={0}, use_global_device_ids=true | all-gather | bytes 14976 | tf_op jit(solution)/shard_map/all_gather | solution.py:133
  95.3 0.8 convolution_bitcast_fusion.1
  96.3 0.8 convolution_bitcast_fusion
  (47 shorter events, 1.5 us)
Async XLA Ops:
  0.6 10.6 %copy-start.1 = (f32[8,8,640]{2,1,0:T(8,128)S(1)}, f32[8,8,640]{2,1,0:T(8,128)}, u32[]{:S(2)}) copy-start(f32[8,8,640]{2,1,0:T(8,128)} %param.9) | copy-start | bytes 491524
  0.6 10.6 %copy-start = (f32[8,8,640]{2,1,0:T(8,128)S(1)}, f32[8,8,640]{2,1,0:T(8,128)}, u32[]{:S(2)}) copy-start(f32[8,8,640]{2,1,0:T(8,128)} %param.10) | copy-start | bytes 491524
  0.7 10.8 %copy-start.4 = (f32[8,8,640]{2,1,0:T(8,128)S(1)}, f32[8,8,640]{2,1,0:T(8,128)}, u32[]{:S(2)}) copy-start(f32[8,8,640]{2,1,0:T(8,128)} %param.11) | copy-start | bytes 491524
  1.6 7.5 %collective-permute-start.1 = (f32[2,2,8,640]{3,2,1,0:T(8,128)S(1)}, f32[2,2,8,640]{3,2,1,0:T(8,128)S(1)}, u32[]{:S(2)}, u32[]{:S(2)}) collective-permute-start(f32[2,2,8,640]{3,2,1,0:T(8,128)S(1)} %get-tuple-element.76), channel_id=1, source_target_pairs={{8,0},{16,8},{24,16},{0,24},{9,1},{17,9},{25,17},{1,25},{10,2},{18... | collective-permute-start | bytes 245768 | tf_op jit(solution)/shard_map/ppermute | solution.py:16
  4.0 5.0 %collective-permute-start = (f32[2,2,8,640]{3,2,1,0:T(8,128)S(1)}, f32[2,2,8,640]{3,2,1,0:T(8,128)S(1)}, u32[]{:S(2)}, u32[]{:S(2)}) collective-permute-start(f32[2,2,8,640]{3,2,1,0:T(8,128)S(1)} %get-tuple-element.77), channel_id=1, source_target_pairs={{0,8},{8,16},{16,24},{24,0},{1,9},{9,17},{17,25},{25,1},{2,10},{10... | collective-permute-start | bytes 245768 | tf_op jit(solution)/shard_map/ppermute | solution.py:15
  11.5 6.0 %collective-permute-start.2 = (f32[2,8,2,640]{3,2,1,0:T(2,128)S(1)}, f32[2,8,2,640]{3,2,1,0:T(2,128)S(1)}, u32[]{:S(2)}, u32[]{:S(2)}) collective-permute-start(f32[2,8,2,640]{3,2,1,0:T(2,128)S(1)} %get-tuple-element.72), channel_id=1, source_target_pairs={{0,1},{1,2},{2,3},{3,4},{4,5},{5,6},{6,7},{8,9},{9,10},{10,11},{11... | collective-permute-start | bytes 245768 | tf_op jit(solution)/shard_map/ppermute | solution.py:15
  14.9 6.7 %collective-permute-start.3 = (f32[2,8,2,640]{3,2,1,0:T(2,128)S(1)}, f32[2,8,2,640]{3,2,1,0:T(2,128)S(1)}, u32[]{:S(2)}, u32[]{:S(2)}) collective-permute-start(f32[2,8,2,640]{3,2,1,0:T(2,128)S(1)} %get-tuple-element.73), channel_id=1, source_target_pairs={{1,0},{2,1},{3,2},{4,3},{5,4},{6,5},{7,6},{9,8},{10,9},{11,10},{12... | collective-permute-start | bytes 245768 | tf_op jit(solution)/shard_map/ppermute | solution.py:16
  16.2 6.2 %copy-start.2 = (f32[8,8,640]{2,1,0:T(8,128)S(1)}, f32[8,8,640]{2,1,0:T(8,128)}, u32[]{:S(2)}) copy-start(f32[8,8,640]{2,1,0:T(8,128)} %param.12) | copy-start | bytes 491524
  21.8 1.0 %copy-start.3 = (s32[8,8,640]{2,1,0:T(8,128)S(1)}, s32[8,8,640]{2,1,0:T(8,128)}, u32[]{:S(2)}) copy-start(s32[8,8,640]{2,1,0:T(8,128)} %param.13) | copy-start | bytes 491524
